TPU v7x, 128 devices: a whole 4x4x4 slice. The times are simulated.
128 devices in a mesh: psg: 32 (over y, z, core), qry: 4 (over x).
Axes of the slice: x: 4, y: 4, z: 4, core: 2. Of those that a mesh axis runs over, the one named last changes fastest.
Arguments:
- queries: bfloat16 [512, 32, 128], P(('psg', 'qry')), may hold values from -6 to 6
- passages: bfloat16 [1024, 256, 128], P('psg'), may hold values from -6 to 6
- candidates: int32 [512, 32], P(('psg', 'qry')), may hold values from 0 to 1023, as said below
- teacher: float32 [512, 32], P(('psg', 'qry')), may hold values from -8 to 8
Outputs:
- pair_loss: float32 [512], P(('psg', 'qry'))
- grad_queries: bfloat16 [512, 32, 128], P(('psg', 'qry'))
- grad_passages: bfloat16 [1024, 256, 128], P('psg', 'qry')
Inputs may be any that keep to these rules, and one draw needn't show every extreme that they name: Passage p lies in block p // 32. Among the 4 x 32 candidates of one device's queries (aligned blocks of 4 rows), at most 10 lie in one passage block; one passage block, the same for all devices, holds exactly 10 of every device's candidates. Candidate ids of one query may repeat.
All inputs are finite; a program needn't handle non-finite values.
Results may differ from a plain program's by a relative error of at most 0.019.
Values may be sent and summed in bfloat16 or wider, within the bound.
A program may use at most 64 MiB of HBM per device.

v0:
```python
import math

import jax
import jax.numpy as jnp
from jax import lax
from jax.sharding import PartitionSpec as P

epsilon = 1e-06
softness_scale = 0.05


def normalize(values):
    widened = values.astype(jnp.float32)
    inverse_norm = lax.rsqrt(jnp.sum(widened * widened, -1, keepdims=True) + epsilon)
    return (widened * inverse_norm, inverse_norm)


def select_rows(row_ids, table):
    row_total = table.shape[0]
    picker = (row_ids[:, None] == lax.iota(jnp.int32, row_total)[None, :]).astype(jnp.bfloat16)
    flat_table = table.reshape(row_total, -1)
    chosen = jnp.dot(picker, flat_table, preferred_element_type=jnp.float32).astype(jnp.bfloat16)
    return chosen.reshape((row_ids.shape[0],) + table.shape[1:])


def add_rows(accum, row_ids, delta):
    row_total = accum.shape[0]
    placer = (row_ids[:, None] == lax.iota(jnp.int32, row_total)[None, :]).astype(jnp.float32)
    flat_delta = delta.reshape(row_ids.shape[0], -1)
    added = jnp.einsum("sr,sx->rx", placer, flat_delta, precision=lax.Precision.HIGHEST)
    return accum + added.reshape(accum.shape)


def shards(queries, passages, candidates, teacher):
    query_count, query_tokens, feature_count = queries.shape
    pass_count, passage_tokens, _ = passages.shape
    cand_count = candidates.shape[1]
    owner_count = lax.axis_size("psg")
    capacity = max(2, (5 * query_count * cand_count + 2 * owner_count - 1) // (2 * owner_count))
    slot_count = owner_count * capacity
    pair_count = query_count * cand_count
    query_unit, query_inverse = normalize(queries)
    passage_unit, passage_inverse = normalize(passages)
    query_norm = query_unit.astype(jnp.bfloat16)
    passage_norm = passage_unit.astype(jnp.bfloat16)
    owner_ids = (candidates // pass_count).reshape(-1)
    local_ids = (candidates % pass_count).reshape(-1)
    onehot = (owner_ids[:, None] == lax.iota(jnp.int32, owner_count)[None, :]).astype(jnp.int32)
    before = jnp.cumsum(onehot, 0) - onehot
    rank_in_owner = jnp.sum(before * onehot, 1)
    slot_ids = owner_ids * capacity + rank_in_owner
    query_local = lax.iota(jnp.int32, pair_count) // cand_count
    slot_code = (
        jnp.zeros((slot_count,), jnp.int32)
        .at[slot_ids]
        .set(query_local * pass_count + local_ids + 1)
    )
    send_code = slot_code.reshape(owner_count, capacity)
    sender = lax.iota(jnp.int32, slot_count) // capacity
    received_label = lax.all_to_all(send_code, "psg", split_axis=0, concat_axis=0, tiled=True)
    query_rows = lax.all_gather(query_norm, "psg", axis=0, tiled=True)
    flat_peek = received_label.reshape(-1)
    fetch_rows = sender * query_count + jnp.where(flat_peek > 0, (flat_peek - 1) // pass_count, 0)
    flat_code = received_label.reshape(-1)
    live = flat_code > 0
    pass_index = jnp.where(live, (flat_code - 1) % pass_count, 0)
    target_rows = sender * query_count + jnp.where(live, (flat_code - 1) // pass_count, 0)
    block_len = math.gcd(slot_count, 64)
    block_total = slot_count // block_len

    def block_terms(offset):
        row_ids = lax.dynamic_slice_in_dim(fetch_rows, offset, block_len)
        passage_ids = lax.dynamic_slice_in_dim(pass_index, offset, block_len)
        query_tile = select_rows(row_ids, query_rows)
        passage_tile = select_rows(passage_ids, passage_norm)
        token_products = jnp.einsum(
            "sqe,spe->sqp", query_tile, passage_tile, preferred_element_type=jnp.float32
        )
        power_value = jnp.exp(token_products / softness_scale)
        return (query_tile, passage_tile, passage_ids, power_value, jnp.sum(power_value, -1))

    def forward_block(offset):
        reduced_sum = block_terms(offset)[4]
        return jnp.sum(softness_scale * jnp.log(reduced_sum), -1)

    offsets = lax.iota(jnp.int32, block_total) * block_len
    slot_scores = lax.map(forward_block, offsets).reshape(owner_count, capacity)
    scores_home = lax.all_to_all(slot_scores, "psg", split_axis=0, concat_axis=0, tiled=True)
    scores = scores_home.reshape(-1)[slot_ids].reshape(query_count, cand_count)
    teacher_exp = jnp.exp(teacher)
    mentor_score_sum = jnp.sum(teacher_exp, -1, keepdims=True)
    target = teacher_exp / mentor_score_sum
    log_target = teacher - jnp.log(mentor_score_sum)
    score_exp = jnp.exp(scores)
    score_total = jnp.sum(score_exp, -1, keepdims=True)
    likelihood = score_exp / score_total
    pair_loss = jnp.sum(target * (log_target - scores), -1) + jnp.log(score_total[:, 0])
    score_grad = likelihood - target
    send_grad = jnp.zeros((slot_count,), jnp.float32).at[slot_ids].set(score_grad.reshape(-1))
    recv_grad = lax.all_to_all(
        send_grad.reshape(owner_count, capacity), "psg", split_axis=0, concat_axis=0, tiled=True
    )
    flat_grad = recv_grad.reshape(-1)

    def backward(step_index, running):
        query_accum, passage_accum = running
        offset = step_index * block_len
        query_tile, passage_tile, passage_ids, power_value, reduced_sum = block_terms(offset)
        slot_grad = lax.dynamic_slice_in_dim(flat_grad, offset, block_len)
        weights = (slot_grad[:, None, None] * power_value / reduced_sum[:, :, None]).astype(
            jnp.bfloat16
        )
        query_delta = jnp.einsum(
            "sqp,spe->sqe", weights, passage_tile, preferred_element_type=jnp.float32
        )
        passage_delta = jnp.einsum(
            "sqp,sqe->spe", weights, query_tile, preferred_element_type=jnp.float32
        )
        home_rows = lax.dynamic_slice_in_dim(target_rows, offset, block_len)
        return (
            add_rows(query_accum, home_rows, query_delta),
            add_rows(passage_accum, passage_ids, passage_delta),
        )

    start_state = (
        jnp.zeros((owner_count * query_count, query_tokens, feature_count), jnp.float32),
        jnp.zeros((pass_count, passage_tokens, feature_count), jnp.float32),
    )
    query_accum, passage_accum = lax.fori_loop(0, block_total, backward, start_state)
    unit_query_grad = lax.psum_scatter(
        query_accum.astype(jnp.bfloat16), "psg", scatter_dimension=0, tiled=True
    ).astype(jnp.float32)
    unit_passage_grad = lax.psum_scatter(
        passage_accum.astype(jnp.bfloat16), "qry", scatter_dimension=1, tiled=True
    ).astype(jnp.float32)
    token_share = unit_passage_grad.shape[1]
    shard_start = lax.axis_index("qry") * token_share
    unit_slice = lax.dynamic_slice_in_dim(passage_unit, shard_start, token_share, 1)
    inverse_slice = lax.dynamic_slice_in_dim(passage_inverse, shard_start, token_share, 1)
    grad_queries = query_inverse * (
        unit_query_grad - query_unit * jnp.sum(query_unit * unit_query_grad, -1, keepdims=True)
    )
    grad_passages = inverse_slice * (
        unit_passage_grad - unit_slice * jnp.sum(unit_slice * unit_passage_grad, -1, keepdims=True)
    )
    return (pair_loss, grad_queries.astype(jnp.bfloat16), grad_passages.astype(jnp.bfloat16))


def solution(mesh):
    placed = (
        P(("psg", "qry"), None, None),
        P("psg", None, None),
        P(("psg", "qry"), None),
        P(("psg", "qry"), None),
    )
    return jax.shard_map(
        shards,
        mesh=mesh,
        in_specs=placed,
        out_specs=(P(("psg", "qry")), P(("psg", "qry"), None, None), P("psg", "qry", None)),
        check_vma=False,
    )
```

profile of v0, /device:TPU:1, one launch (start us, length us, event | category | flops | bytes accessed | tf_op | source)
XLA Modules:
  0.0 386.0 jit_solution(9751753425798929386)
XLA Ops:
  12.7 9.6 %all-to-all-start = ((s32[32,1,10]{2,1,0:T(1,128)}), s32[32,1,10]{2,1,0:T(1,128)S(1)}, u32[]{:S(2)}, u32[]{:S(2)}) async-start(s32[32,1,10]{2,1,0:T(1,128)} %bitcast.4), calls=%async_computation | async-start | bytes 32768 | tf_op jit(solution)/shard_map/all_to_all | solution.py:60
  22.3 2.9 fusion.34
  25.2 3.1 convert_multiply_fusion
  29.5 27.6 %all-gather.2.cloned.1.call-done = bf16[128,32,128]{2,1,0:T(8,128)(2,1)} async-done(((bf16[4,32,128]{2,1,0:T(8,128)(2,1)}), bf16[128,32,128]{2,1,0:T(8,128)(2,1)}) %all-gather.2.cloned.1.call-update) | async-done | bytes 1048592 | tf_op jit(solution)/shard_map/all_gather | solution.py:61
  57.1 44.8 %while.27 = (s32[]{:T(128)}, f32[5,64]{1,0:T(8,128)S(1)}, s32[5]{0:T(128)S(1)}, s32[320]{0:T(512)S(1)}, bf16[128,32,128]{2,1,0:T(8,128)(2,1)}, /*index=5*/s32[32...) while((s32[]{:T(128)}, f32[5,64]{1,0:T(8,128)S(1)}, s32[5]{0:T(128)S(1)}, ...), condition=%wide.region_9.10_spmd, body=%wide.region_6.9_spmd.sunk | while | flops 338964416 | bytes 22055336 | solution.py:87
  102.6 5.3 %all-to-all-start.1 = ((f32[32,1,10]{2,1,0:T(1,128)}), f32[32,1,10]{2,1,0:T(1,128)S(1)}, u32[]{:S(2)}, u32[]{:S(2)}) async-start(f32[32,1,10]{2,1,0:T(1,128)} %bitcast.5), calls=%async_computation.1 | async-start | bytes 32768 | tf_op jit(solution)/shard_map/all_to_all | solution.py:88
  108.1 6.8 %all-to-all-done.1 = f32[32,1,10]{2,1,0:T(1,128)S(1)} async-done(((f32[32,1,10]{2,1,0:T(1,128)}), f32[32,1,10]{2,1,0:T(1,128)S(1)}, u32[]{:S(2)}, u32[]{:S(2)}) %all-to-all-start.1) | async-done | bytes 1312 | tf_op jit(solution)/shard_map/all_to_all | solution.py:88
  119.6 4.1 %all-to-all-start.2 = ((f32[32,1,10]{2,1,0:T(1,128)}), f32[32,1,10]{2,1,0:T(1,128)S(1)}, u32[]{:S(2)}, u32[]{:S(2)}) async-start(f32[32,1,10]{2,1,0:T(1,128)} %bitcast.6), calls=%async_computation.2 | async-start | bytes 32768 | tf_op jit(solution)/shard_map/all_to_all | solution.py:100
  123.8 6.9 %all-to-all-done.2 = f32[32,1,10]{2,1,0:T(1,128)S(1)} async-done(((f32[32,1,10]{2,1,0:T(1,128)}), f32[32,1,10]{2,1,0:T(1,128)S(1)}, u32[]{:S(2)}, u32[]{:S(2)}) %all-to-all-start.2) | async-done | bytes 1312 | tf_op jit(solution)/shard_map/all_to_all | solution.py:100
  131.5 131.0 %while.28 = (s32[]{:T(128)}, f32[128,32,128]{2,0,1:T(8,128)}, f32[32,256,128]{2,0,1:T(8,128)}, s32[320]{0:T(512)S(1)}, f32[320]{0:T(512)S(1)}, /*index=5*/bf16[1...) while((s32[]{:T(128)}, f32[128,32,128]{2,0,1:T(8,128)}, ...), condition=%wide.region_15.16_spmd.clone, body=%wide.region_13.15_spmd.clone.sunk | while | flops 1822705664 | bytes 114847024 | solution.py:129
  145.3 10.6 %select_add_fusion.5 = f32[32,256,128]{2,0,1:T(8,128)S(1)} fusion(f32[32,256,128]{2,0,1:T(8,128)S(1)} %copy-done, pred[]{:T(512)S(6)} %compare.11, s32[64]{0:T(128)S(1)} %dynamic_slice.59, f32[8,8,256,128]{3,2,1,0:T(8,128)S(1)} %bitcast.149), kind=kOutput, calls=%fused_computation.23.clone.1 | convolution fusion | flops 807405568 | bytes 16777472 | tf_op jit(solution)/shard_map/while/body/eval_jaxpr/sr,sx->rx/dot_general | solution.py:30
  165.8 2.7 select_add_fusion.4
  171.4 10.6 %select_add_fusion.5 = f32[32,256,128]{2,0,1:T(8,128)S(1)} fusion(f32[32,256,128]{2,0,1:T(8,128)S(1)} %copy-done, pred[]{:T(512)S(6)} %compare.11, s32[64]{0:T(128)S(1)} %dynamic_slice.59, f32[8,8,256,128]{3,2,1,0:T(8,128)S(1)} %bitcast.149), kind=kOutput, calls=%fused_computation.23.clone.1 | convolution fusion | flops 807405568 | bytes 16777472 | tf_op jit(solution)/shard_map/while/body/eval_jaxpr/sr,sx->rx/dot_general | solution.py:30
  192.0 2.7 select_add_fusion.4
  197.6 10.6 %select_add_fusion.5 = f32[32,256,128]{2,0,1:T(8,128)S(1)} fusion(f32[32,256,128]{2,0,1:T(8,128)S(1)} %copy-done, pred[]{:T(512)S(6)} %compare.11, s32[64]{0:T(128)S(1)} %dynamic_slice.59, f32[8,8,256,128]{3,2,1,0:T(8,128)S(1)} %bitcast.149), kind=kOutput, calls=%fused_computation.23.clone.1 | convolution fusion | flops 807405568 | bytes 16777472 | tf_op jit(solution)/shard_map/while/body/eval_jaxpr/sr,sx->rx/dot_general | solution.py:30
  218.1 2.7 select_add_fusion.4
  223.7 10.6 %select_add_fusion.5 = f32[32,256,128]{2,0,1:T(8,128)S(1)} fusion(f32[32,256,128]{2,0,1:T(8,128)S(1)} %copy-done, pred[]{:T(512)S(6)} %compare.11, s32[64]{0:T(128)S(1)} %dynamic_slice.59, f32[8,8,256,128]{3,2,1,0:T(8,128)S(1)} %bitcast.149), kind=kOutput, calls=%fused_computation.23.clone.1 | convolution fusion | flops 807405568 | bytes 16777472 | tf_op jit(solution)/shard_map/while/body/eval_jaxpr/sr,sx->rx/dot_general | solution.py:30
  244.3 2.7 select_add_fusion.4
  249.9 10.6 %select_add_fusion.5 = f32[32,256,128]{2,0,1:T(8,128)S(1)} fusion(f32[32,256,128]{2,0,1:T(8,128)S(1)} %copy-done, pred[]{:T(512)S(6)} %compare.11, s32[64]{0:T(128)S(1)} %dynamic_slice.59, f32[8,8,256,128]{3,2,1,0:T(8,128)S(1)} %bitcast.149), kind=kOutput, calls=%fused_computation.23.clone.1 | convolution fusion | flops 807405568 | bytes 16777472 | tf_op jit(solution)/shard_map/while/body/eval_jaxpr/sr,sx->rx/dot_general | solution.py:30
  262.5 3.8 copy.86
  266.3 6.0 %copy.85 = bf16[32,256,128]{2,1,0:T(8,128)(2,1)} copy(f32[32,256,128]{2,0,1:T(8,128)} %get-tuple-element.206) | data formatting | bytes 6291456 | tf_op jit(solution)/shard_map/while | solution.py:129
  273.0 67.0 %reduce-scatter.3.cloned.1.call-done = bf16[4,32,128]{2,1,0:T(8,128)(2,1)} async-done(((bf16[128,32,128]{2,1,0:T(8,128)(2,1)}), bf16[4,32,128]{2,1,0:T(8,128)(2,1)}) %reduce-scatter.3.cloned.1.call-update) | async-done | bytes 32784 | tf_op jit(solution)/shard_map/reduce_scatter | solution.py:130
  342.0 31.2 %reduce-scatter.5.cloned.1.call-done = bf16[32,64,128]{2,1,0:T(8,128)(2,1)} async-done(((bf16[32,256,128]{2,1,0:T(8,128)(2,1)}), bf16[32,64,128]{2,1,0:T(8,128)(2,1)}) %reduce-scatter.5.cloned.1.call-update) | async-done | bytes 524304 | tf_op jit(solution)/shard_map/reduce_scatter | solution.py:133
  373.2 6.3 %fusion.39 = bf16[32,64,128]{2,1,0:T(8,128)(2,1)} fusion(bf16[32,64,128]{2,1,0:T(8,128)(2,1)} %reduce-scatter.5.cloned.1.call-done, f32[32,256,128]{2,1,0:T(8,128)} %get-tuple-element.270, s32[]{:T(128)S(6)} %select_n.80, f32[32,64]{1,0:T(8,128)S(1)} %constant_dynamic-slice_fusion), kind=kOutput, calls=%fused_computation.59 | output fusion | flops 1837183 | bytes 3679232 | tf_op jit(solution)/shard_map/mul | solution.py:144
  (202 shorter events, 117.1 us)
Async XLA Ops:
  7.2 50.0 %all-gather.2.cloned.1.call-start = ((), (), s32[]{:S(2)}) async-start(), calls=%async_computation.5 | async-start | bytes 1081344 | tf_op jit(solution)/shard_map/all_gather | solution.py:61
  12.7 16.5 %all-to-all-start = ((s32[32,1,10]{2,1,0:T(1,128)}), s32[32,1,10]{2,1,0:T(1,128)S(1)}, u32[]{:S(2)}, u32[]{:S(2)}) async-start(s32[32,1,10]{2,1,0:T(1,128)} %bitcast.4), calls=%async_computation | async-start | bytes 32768 | tf_op jit(solution)/shard_map/all_to_all | solution.py:60
  22.3 3.0 copy-start.4
  57.1 50.8 %copy-start.6 = (f32[4,32]{1,0:T(4,128)S(1)}, f32[4,32]{1,0:T(4,128)}, u32[]{:S(2)}) copy-start(f32[4,32]{1,0:T(4,128)} %param.11) | copy-start | bytes 1540
  102.6 12.2 %all-to-all-start.1 = ((f32[32,1,10]{2,1,0:T(1,128)}), f32[32,1,10]{2,1,0:T(1,128)S(1)}, u32[]{:S(2)}, u32[]{:S(2)}) async-start(f32[32,1,10]{2,1,0:T(1,128)} %bitcast.5), calls=%async_computation.1 | async-start | bytes 32768 | tf_op jit(solution)/shard_map/all_to_all | solution.py:88
  119.6 11.2 %all-to-all-start.2 = ((f32[32,1,10]{2,1,0:T(1,128)}), f32[32,1,10]{2,1,0:T(1,128)S(1)}, u32[]{:S(2)}, u32[]{:S(2)}) async-start(f32[32,1,10]{2,1,0:T(1,128)} %bitcast.6), calls=%async_computation.2 | async-start | bytes 32768 | tf_op jit(solution)/shard_map/all_to_all | solution.py:100
  123.7 216.3 %reduce-scatter.3.cloned.1.call-start = ((), (), s32[]{:S(2)}) async-start(), calls=%async_computation.6 | async-start | bytes 1081344 | tf_op jit(solution)/shard_map/reduce_scatter | solution.py:130
  142.3 1.9 copy-start.3
  142.3 2.9 copy-start
  155.9 2.0 copy-start.1
  168.5 1.9 copy-start.3
  168.5 2.9 copy-start
  182.0 2.0 copy-start.1
  194.6 1.9 copy-start.3
  194.6 2.9 copy-start
  208.2 2.0 copy-start.1
  220.8 1.9 copy-start.3
  220.8 2.9 copy-start
  234.4 2.0 copy-start.1
  246.9 1.9 copy-start.3
  246.9 2.9 copy-start
  260.5 2.0 copy-start.1
  266.3 106.9 %reduce-scatter.5.cloned.1.call-start = ((), (), s32[]{:S(2)}) async-start(), calls=%async_computation.7 | async-start | bytes 2621440 | tf_op jit(solution)/shard_map/reduce_scatter | solution.py:133
  272.4 67.7 %copy-start.5 = (bf16[4,32,128]{2,1,0:T(8,128)(2,1)S(1)}, bf16[4,32,128]{2,1,0:T(8,128)(2,1)}, u32[]{:S(2)}) copy-start(bf16[4,32,128]{2,1,0:T(8,128)(2,1)} %param.8) | copy-start | bytes 98308
  (5 other events, 8.0 us)
Sparse Core Ops, SparseCore 0:
  10.8 46.2 all-gather.1
  266.4 73.5 reduce-scatter.2
  342.4 30.7 reduce-scatter.4
where the time goes:
time: 388 us; the launch traced here: 386 us
  waiting for transfers between devices  140 us (36%)
  matrix products  129 us (33%)
  local copies, waits for them, and re-layouts  53 us (14%)
  other arithmetic  20.3 us (5%)
  starting transfers between devices  19.1 us (5%)
  between operations  14 us (4%)
  loops' own time  10.6 us (3%)
    reduce_scatter x1, waiting for transfers between devices, shards(): lax.psum_scatter(query_accum.astype(jnp.bfloat16), 'psg', scatter_dimensi...  67 us
    dot_general x10, matrix products, add_rows(): jnp.einsum('sr,sx->rx', placer, flat_delta, precision=lax.Precision.HIGHEST)  66.4 us
    dot_general x20, matrix products, select_rows(): jnp.dot(picker, flat_table, preferred_element_type=jnp.float32)  32.2 us
    reduce_scatter x1, waiting for transfers between devices, shards(): lax.psum_scatter(passage_accum.astype(jnp.bfloat16), 'qry', scatter_dimen...  31.2 us
    while x60, local copies, waits for them, and re-layouts  31.1 us
    all_gather x1, waiting for transfers between devices, shards(): query_rows = lax.all_gather(query_norm, 'psg', axis=0, tiled=True)  27.6 us
    dot_general x10, matrix products, block_terms(): jnp.einsum('sqe,spe->sqp', query_tile, passage_tile, preferred_element_ty...  16.2 us
    another operation x1, loops' own time, shards(): slot_scores = lax.map(forward_block, offsets).reshape(owner_count, capacity)  9.92 us
  transfers between devices with their start and end apart: 6, of which 6 were waited for; matrix products, arithmetic and copies ran while one was open for 5% of the time, Pallas kernels for 0%

commit v1 on v0

v1 whole, which is shorter than its diff:
```python
import math

import jax
import jax.numpy as jnp
from jax import lax
from jax.experimental import pallas as pl
from jax.experimental.pallas import tpu as pltpu
from jax.sharding import PartitionSpec as P

MESH = pl.DeviceIdType.MESH
BF16, F32, I32 = jnp.bfloat16, jnp.float32, jnp.int32
HIGHEST = lax.Precision.HIGHEST
epsilon = 1e-06
softness_scale = 0.05

OWNERS, GROUPS, CHIPS = 32, 4, 16
QD, QT, C, E, PT, PS = 4, 32, 32, 128, 256, 32
CAP = 10
ROW = QD * QT
SHARE = PT // GROUPS
PER_CHUNK = 4
CHUNKS = (OWNERS * CAP + PS * (PER_CHUNK - 1)) // PER_CHUNK
UNROLL = 4
STEPS = CHUNKS // UNROLL
SLOTS = 512
LANES_PER_SENDER = SLOTS // OWNERS
ORDER = (2, 1, 3, 0)

NT = (((1,), (1,)), ((), ()))
TN = (((0,), (0,)), ((), ()))


def iota(shape, dim):
    return lax.broadcasted_iota(I32, shape, dim)


def dot(a, b, dims=None, precision=None):
    dims = (((1,), (0,)), ((), ())) if dims is None else dims
    return lax.dot_general(a, b, dims, precision=precision, preferred_element_type=F32)


def unit_of(values):
    inverse = lax.rsqrt(jnp.sum(values * values, -1, keepdims=True) + epsilon)
    return values * inverse, inverse


def project(values, gradient):
    unit, inverse = unit_of(values)
    return inverse * (gradient - unit * jnp.sum(unit * gradient, -1, keepdims=True))


def count(mask, axis):
    return jnp.sum(jnp.where(mask, 1, 0), axis, keepdims=True)


def same(a, b):
    return (1 - jnp.minimum((a - b) * (a - b), 1)).astype(F32)


def column_of(row):
    return jnp.broadcast_to(row, (ROW, row.shape[1])).T[:, 0:1]


def slot_tables(ids, teacher):
    lane = iota((1, ROW), 1)
    power = jnp.exp(teacher)
    same_query = (iota((ROW, ROW), 0) // C == iota((ROW, ROW), 1) // C).astype(F32)
    power_sum = dot(jnp.broadcast_to(power, (8, ROW)), same_query, precision=HIGHEST)[0:1]
    target = power / power_sum
    owner = ids >> 5
    code = (lane >> 5) * PS + (ids & (PS - 1)) + 1
    ahead = iota((ROW, ROW), 0) < iota((ROW, ROW), 1)
    rank = count((column_of(owner) == owner) & ahead, 0)
    hits = owner == iota((OWNERS, ROW), 0)
    place = iota((OWNERS, ROW), 1) & (LANES_PER_SENDER - 1)
    codes = jnp.zeros((OWNERS, ROW), I32)
    targets = jnp.zeros((OWNERS, ROW), F32)
    for slot in range(CAP):
        chosen = hits & (rank == slot)
        codes = jnp.where(place == slot, jnp.sum(jnp.where(chosen, code, 0), 1, keepdims=True), codes)
        targets = jnp.where(place == slot, jnp.sum(jnp.where(chosen, target, 0.0), 1, keepdims=True), targets)
    return codes, targets


def order_slots(codes, targets):
    lane = iota((OWNERS, SLOTS), 1)
    mine = lane >> 4 == iota((OWNERS, SLOTS), 0)
    code = jnp.sum(jnp.where(mine, jnp.concatenate([codes] * 4, 1), 0), 0, keepdims=True) - 1
    target = jnp.sum(jnp.where(mine, jnp.concatenate([targets] * 4, 1), 0.0), 0, keepdims=True)
    live = code >= 0
    local = code >> 5
    query = (iota((1, SLOTS), 1) >> 4) * QD + local
    passage = jnp.where(live, code & (PS - 1), -1)
    ahead = iota((SLOTS, SLOTS), 0) < iota((SLOTS, SLOTS), 1)
    rank = count((column_of(passage) == passage) & ahead, 0)
    index = iota((PS, SLOTS), 0)
    hits = passage == index
    chunks = (count(hits, 1) + (PER_CHUNK - 1)) >> 2
    chunk_row = jnp.sum(jnp.where(lane == index, chunks, 0), 0, keepdims=True)
    first = jnp.sum(jnp.where(lane < index, chunk_row, 0), 1, keepdims=True)
    place = rank + PER_CHUNK * jnp.sum(jnp.where(hits, first, 0), 0, keepdims=True)
    place = jnp.where(live, place, -1)
    ordered = column_of(place) == iota((SLOTS, SLOTS), 1)
    ordered = jnp.sum(jnp.where(ordered, column_of(query) + 1, 0), 0, keepdims=True) - 1
    inside = (first <= lane) & (lane < first + chunks)
    chunk_passage = jnp.sum(jnp.where(inside, index, 0), 0, keepdims=True)
    last = jnp.where(lane == index, jnp.maximum(first + chunks - 1, 0), 0)
    last = jnp.where(lane == index + ROW, jnp.minimum(chunks, 1), last)
    meta = [
        jnp.maximum(ordered, 0),
        chunk_passage,
        jnp.maximum(place, 0),
        jnp.where(live, local, -1),
        jnp.sum(last, 0, keepdims=True),
        ordered,
    ]
    chosen = (iota((SLOTS, SLOTS), 0) == place).astype(BF16)
    high = target.astype(BF16).astype(F32)
    middle = (target - high).astype(BF16).astype(F32)
    low = target - high - middle
    pick = iota((ROW, SLOTS), 0)
    values = jnp.zeros((ROW, SLOTS), F32)
    for row_index, row in enumerate((query.astype(F32), live.astype(F32), high, middle, low)):
        values = jnp.where(pick == row_index, row, values)
    return meta, dot(chosen, values.astype(BF16), NT)


def kernel(
    q_ref, ids_ref, teacher_ref, passages_hbm,
    total_out, gq_out, gp_out,
    q_all, raw, p_norm, code_out, code_in, target_out, target_in, meta_v, meta_s, column, exps_a, exps_b, terms, scaled,
    scores, grads, sums_out, sums_in, part_a, part_b, r2, r1, r3, in_left, in_right, from_left, from_right,
    g_sib_out, g_sib_in, g_out, g_in,
    local_sem, q_send, q_recv, relay_send, relay_recv, code_send, code_recv, target_send, target_recv,
    sums_send, sums_recv, x_send, x_recv, sib_send, sib_recv, g_send, g_recv,
):
    me = lax.axis_index("psg")
    col = lax.axis_index("qry")
    chip, core = me // 2, me % 2
    sibling = chip * 2 + (1 - core)
    right, left = (col + 1) % GROUPS, (col + GROUPS - 1) % GROUPS

    def peer(step):
        return (me + step) % OWNERS

    barrier = pltpu.get_barrier_semaphore()

    def greet(step, carry):
        pl.semaphore_signal(barrier, inc=1, device_id={"psg": peer(step)}, device_id_type=MESH)
        return carry

    lax.fori_loop(1, OWNERS, greet, 0)
    for side in (left, right):
        pl.semaphore_signal(barrier, inc=1, device_id={"qry": side}, device_id_type=MESH)

    loads = []
    for index, relative in enumerate(ORDER):
        share = (col + relative) % GROUPS
        load = pltpu.make_async_copy(
            passages_hbm.at[:, pl.ds(pl.multiple_of(share * SHARE, SHARE), SHARE), :],
            raw.at[:, pl.ds(index * SHARE, SHARE), :],
            local_sem.at[index],
        )
        load.start()
        loads.append(load)

    q_raw = q_ref[...].astype(F32)
    own_rows = pl.ds(me * QD, QD)
    q_all[own_rows] = unit_of(q_raw)[0].astype(BF16).reshape(QD, QT, E)
    codes, targets = slot_tables(ids_ref[...], teacher_ref[...])
    for owner in range(OWNERS):
        code_out[owner] = codes[owner : owner + 1]
        target_out[owner] = targets[owner : owner + 1]
    code_in[me] = code_out[me]
    target_in[me] = target_out[me]

    pl.semaphore_wait(barrier, OWNERS - 1 + 2)

    def send_table(step, carry):
        pltpu.make_async_remote_copy(
            src_ref=code_out.at[peer(step)], dst_ref=code_in.at[me], send_sem=code_send, recv_sem=code_recv,
            device_id={"psg": peer(step)}, device_id_type=MESH,
        ).start()
        pltpu.make_async_remote_copy(
            src_ref=target_out.at[peer(step)], dst_ref=target_in.at[me], send_sem=target_send, recv_sem=target_recv,
            device_id={"psg": peer(step)}, device_id_type=MESH,
        ).start()
        return carry

    lax.fori_loop(1, OWNERS, send_table, 0)

    def send_query(step, carry):
        pltpu.make_async_remote_copy(
            src_ref=q_all.at[own_rows], dst_ref=q_all.at[own_rows], send_sem=q_send, recv_sem=q_recv.at[chip],
            device_id={"psg": ((chip + step) % CHIPS) * 2 + core}, device_id_type=MESH,
        ).start()
        return carry

    lax.fori_loop(1, CHIPS, send_query, 0)

    def relay(rows):
        return pltpu.make_async_remote_copy(
            src_ref=q_all.at[rows], dst_ref=q_all.at[rows], send_sem=relay_send, recv_sem=relay_recv,
            device_id={"psg": sibling}, device_id_type=MESH,
        )

    relay(own_rows).start()

    for load in loads:
        load.wait()

    def normalize(index, carry):
        values = raw[index].astype(F32)
        p_norm[index] = unit_of(values)[0].astype(BF16)
        return carry

    lax.fori_loop(0, PS, normalize, 0, unroll=4)

    others = pl.ds(0, OWNERS - 1)
    pltpu.make_async_copy(code_in.at[others], code_in.at[others], code_recv).wait()
    pltpu.make_async_copy(target_in.at[others], target_in.at[others], target_recv).wait()
    meta, by_column = order_slots(
        jnp.concatenate([code_in[owner] for owner in range(OWNERS)], 0),
        jnp.concatenate([target_in[owner] for owner in range(OWNERS)], 0),
    )
    for index, row in enumerate(meta):
        meta_v[index : index + 1, :] = row
    meta_v[6:8, :] = jnp.zeros((2, SLOTS), I32)
    column[...] = by_column
    scores[...] = jnp.zeros_like(scores)

    def hand_on(step, carry):
        sender = (chip + CHIPS - step) % CHIPS
        rows = pl.ds((sender * 2 + core) * QD, QD)
        pltpu.make_async_copy(q_all.at[rows], q_all.at[rows], q_recv.at[sender]).wait()
        relay(rows).start()
        return carry

    lax.fori_loop(1, CHIPS, hand_on, 0)
    to_scalar = pltpu.make_async_copy(meta_v, meta_s, local_sem.at[4])
    to_scalar.start()
    to_scalar.wait()
    half = pl.ds(0, CHIPS * QD)
    pltpu.make_async_copy(q_all.at[half], q_all.at[half], relay_recv).wait()

    factor = math.log2(math.e) / softness_scale
    ones = jnp.ones((PT, E), BF16)

    def forward(step, carry):
        lines = []
        for inner in range(UNROLL):
            chunk = step * UNROLL + inner
            rows = pl.ds(pl.multiple_of(chunk * ROW, ROW), ROW)
            passage = meta_s[1, chunk]
            tokens = p_norm[passage]
            queries = jnp.concatenate(
                [
                    q_all[meta_s[0, chunk * PER_CHUNK + slot]]
                    for slot in range(PER_CHUNK)
                ],
                0,
            )
            power = jnp.exp2(dot(queries, tokens, NT) * factor).astype(BF16)
            exps_a[rows, :] = power[:, : PT // 2]
            exps_b[rows, :] = power[:, PT // 2 :]
            both = dot(power, jnp.concatenate([tokens, ones], 1))
            total = both[:, E:]
            inverse = 1.0 / total
            terms[pl.ds(chunk * PER_CHUNK, PER_CHUNK)] = (
                (both[:, :E] * inverse).astype(BF16).reshape(PER_CHUNK, QT, E)
            )
            scaled[rows, :] = (queries.astype(F32) * inverse).astype(BF16)
            logs = jnp.log(total)
            for slot in range(PER_CHUNK):
                lines.append(jnp.sum(logs[slot * QT : (slot + 1) * QT], 0, keepdims=True))
        line_count = UNROLL * PER_CHUNK
        lines = jnp.concatenate(lines, 0) * softness_scale
        scores[pl.ds(pl.multiple_of(step * line_count, line_count), line_count), :] = lines
        return carry

    lax.fori_loop(0, STEPS, forward, 0)

    query_row = meta_v[5:6, :]
    live = column[:, 1:2] > 0.5
    target = column[:, 2:3] + column[:, 3:4] + column[:, 4:5]
    score = scores[...]
    power = jnp.exp(score)
    lane = iota((SLOTS, ROW), 1)
    summands = jnp.where(live, jnp.where(lane < ROW // 2, power, target * score), 0.0)
    belongs = (query_row == iota((ROW, SLOTS), 0)).astype(F32)
    partial = dot(belongs, summands, precision=HIGHEST).T
    sums_out[0:1, :] = partial[0:1]
    sums_out[1:2, :] = partial[ROW // 2 : ROW // 2 + 1]
    sums_in[me] = sums_out[...]

    def send_sums(step, carry):
        pltpu.make_async_remote_copy(
            src_ref=sums_out, dst_ref=sums_in.at[me], send_sem=sums_send, recv_sem=sums_recv,
            device_id={"psg": peer(step)}, device_id_type=MESH,
        ).start()
        return carry

    lax.fori_loop(1, OWNERS, send_sums, 0)
    pltpu.make_async_copy(sums_in.at[others], sums_in.at[others], sums_recv).wait()
    totals = sums_in[0]
    for owner in range(1, OWNERS):
        totals = totals + sums_in[owner]
    total_row = totals[0:1]
    total_out[...] = jnp.log(total_row) - totals[1:2]
    own_query = column[:, 0:1].astype(I32) == lane
    total_here = jnp.sum(jnp.where(own_query, total_row, 0.0), 1, keepdims=True)
    grads[...] = jnp.where(live, power / jnp.where(live, total_here, 1.0) - target, 0.0)

    def passage_step(first, exps, parts):
        def run(step, running):
            line_count = UNROLL * PER_CHUNK
            grad_rows = grads[pl.ds(pl.multiple_of(step * line_count, line_count), line_count), :] if first else None
            for inner in range(UNROLL):
                chunk = step * UNROLL + inner
                rows = pl.ds(pl.multiple_of(chunk * ROW, ROW), ROW)
                here = meta_s[1, chunk]
                before = meta_s[1, jnp.maximum(chunk - 1, 0)]
                keep = same(here, before)
                if first:
                    weight = jnp.concatenate(
                        [
                            jnp.broadcast_to(grad_rows[inner * PER_CHUNK + slot][None, :], (QT, E))
                            for slot in range(PER_CHUNK)
                        ],
                        0,
                    )
                    side = (scaled[rows, :].astype(F32) * weight).astype(BF16)
                    scaled[rows, :] = side
                else:
                    side = scaled[rows, :]
                running = running * keep + dot(exps[rows, :], side, TN)
                parts[chunk] = running.astype(BF16)
            return running

        lax.fori_loop(0, STEPS, run, jnp.zeros((2 * SHARE, E), F32))

    def last_part(parts, index, begin):
        used = meta_s[4, ROW + index].astype(F32)
        return parts[meta_s[4, index]][begin : begin + SHARE].astype(F32) * used

    def collect(parts, begin, out):
        def run(index, carry):
            out[index] = last_part(parts, index, begin).astype(BF16)
            return carry

        lax.fori_loop(0, PS, run, 0, unroll=4)

    def send_x(index, side, source, target_ref):
        copy = pltpu.make_async_remote_copy(
            src_ref=source, dst_ref=target_ref, send_sem=x_send.at[index], recv_sem=x_recv.at[index],
            device_id={"qry": side}, device_id_type=MESH,
        )
        copy.start()
        return copy

    low, high = pl.ds(0, PS // 2), pl.ds(PS // 2, PS // 2)
    passage_step(True, exps_a, part_a)
    collect(part_a, 0, r2)
    onward_right = send_x(0, right, r2.at[low], in_left)
    onward_left = send_x(1, left, r2.at[high], in_right)
    collect(part_a, SHARE, r1)
    direct_right = send_x(2, right, r1.at[high], from_left.at[high])
    passage_step(False, exps_b, part_b)
    collect(part_b, 0, r3)
    direct_left = send_x(3, left, r3.at[low], from_right.at[low])

    def query_block(sender):
        sums = [jnp.zeros((QT, E), F32) for _ in range(QD)]
        for slot in range(CAP):
            index = sender * LANES_PER_SENDER + slot
            place = meta_s[2, index]
            local = meta_s[3, index]
            term = terms[place].astype(F32) * grads[pl.ds(place, 1), :]
            for query in range(QD):
                sums[query] = sums[query] + term * same(local, query)
        return jnp.concatenate(sums, 0)

    def for_sibling(index, carry):
        g_sib_out[index] = query_block(index * 2 + (1 - core)).astype(BF16)
        return carry

    def for_chips(index, carry):
        g_out[index] = query_block(index * 2 + core).astype(BF16)
        return carry

    lax.fori_loop(0, CHIPS, for_sibling, 0)
    to_sibling = pltpu.make_async_remote_copy(
        src_ref=g_sib_out, dst_ref=g_sib_in, send_sem=sib_send, recv_sem=sib_recv,
        device_id={"psg": sibling}, device_id_type=MESH,
    )
    to_sibling.start()
    lax.fori_loop(0, CHIPS, for_chips, 0)
    to_sibling.wait_recv()

    def add_sibling(index, carry):
        g_out[index] = (g_out[index].astype(F32) + g_sib_in[index].astype(F32)).astype(BF16)
        return carry

    lax.fori_loop(0, CHIPS, add_sibling, 0)

    def send_grad(step, carry):
        other = (chip + step) % CHIPS
        pltpu.make_async_remote_copy(
            src_ref=g_out.at[other], dst_ref=g_in.at[chip], send_sem=g_send, recv_sem=g_recv,
            device_id={"psg": other * 2 + core}, device_id_type=MESH,
        ).start()
        return carry

    lax.fori_loop(1, CHIPS, send_grad, 0)
    g_in[chip] = g_out[chip]

    def merge(incoming, out, begin):
        def run(index, carry):
            both = out[begin + index].astype(F32) + incoming[index].astype(F32)
            out[begin + index] = both.astype(BF16)
            return carry

        lax.fori_loop(0, PS // 2, run, 0, unroll=4)

    onward_right.wait_recv()
    merge(in_left, r1, 0)
    final_right = send_x(4, right, r1.at[low], from_left.at[low])
    onward_left.wait_recv()
    merge(in_right, r3, PS // 2)
    final_left = send_x(5, left, r3.at[high], from_right.at[high])

    fewer = pl.ds(0, CHIPS - 1)
    pltpu.make_async_copy(g_in.at[fewer], g_in.at[fewer], g_recv).wait()
    gradient = jnp.zeros((ROW, E), F32)
    for index in range(CHIPS):
        gradient = gradient + g_in[index].astype(F32)
    gq_out[...] = project(q_ref[...].astype(F32), gradient).astype(BF16)

    for copy in (direct_right, direct_left, final_right, final_left):
        copy.wait_recv()

    def finish(index, carry):
        gradient = last_part(part_b, index, SHARE)
        gradient = gradient + from_left[index].astype(F32) + from_right[index].astype(F32)
        values = raw[index, 3 * SHARE : 4 * SHARE, :].astype(F32)
        gp_out[index] = project(values, gradient).astype(BF16)
        return carry

    lax.fori_loop(0, PS, finish, 0, unroll=4)

    for copy in (onward_right, onward_left, direct_right, direct_left, final_right, final_left, to_sibling):
        copy.wait_send()
    pltpu.make_async_copy(code_in.at[others], code_in.at[others], code_send).wait()
    pltpu.make_async_copy(target_in.at[others], target_in.at[others], target_send).wait()
    pltpu.make_async_copy(sums_in.at[others], sums_in.at[others], sums_send).wait()
    pltpu.make_async_copy(g_in.at[fewer], g_in.at[fewer], g_send).wait()
    sent = pl.ds(0, (CHIPS - 1) * QD)
    pltpu.make_async_copy(q_all.at[sent], q_all.at[sent], q_send).wait()
    pltpu.make_async_copy(q_all.at[half], q_all.at[half], relay_send).wait()


def step(queries, ids, teacher, passages):
    dma = pltpu.SemaphoreType.DMA
    vmem = pltpu.VMEM
    rows = CHUNKS * ROW
    share = (PS, SHARE, E)
    half_share = (PS // 2, SHARE, E)
    return pl.pallas_call(
        kernel,
        out_shape=(
            jax.ShapeDtypeStruct((1, ROW), F32),
            jax.ShapeDtypeStruct((ROW, E), BF16),
            jax.ShapeDtypeStruct(share, BF16),
        ),
        in_specs=[pl.BlockSpec(memory_space=pltpu.VMEM)] * 3 + [pl.BlockSpec(memory_space=pl.ANY)],
        out_specs=(pl.BlockSpec(memory_space=pltpu.VMEM),) * 3,
        scratch_shapes=[
            vmem((OWNERS * QD, QT, E), BF16),
            vmem((PS, PT, E), BF16),
            vmem((PS, PT, E), BF16),
            vmem((OWNERS, 1, ROW), I32),
            vmem((OWNERS, 1, ROW), I32),
            vmem((OWNERS, 1, ROW), F32),
            vmem((OWNERS, 1, ROW), F32),
            vmem((8, SLOTS), I32),
            pltpu.SMEM((8, SLOTS), I32),
            vmem((SLOTS, ROW), F32),
            vmem((rows, PT // 2), BF16),
            vmem((rows, PT // 2), BF16),
            vmem((CHUNKS * PER_CHUNK, QT, E), BF16),
            vmem((rows, E), BF16),
            vmem((SLOTS, ROW), F32),
            vmem((SLOTS, ROW), F32),
            vmem((2, ROW), F32),
            vmem((OWNERS, 2, ROW), F32),
            vmem((CHUNKS, 2 * SHARE, E), BF16),
            vmem((CHUNKS, 2 * SHARE, E), BF16),
            vmem(share, BF16),
            vmem(share, BF16),
            vmem(share, BF16),
            vmem(half_share, BF16),
            vmem(half_share, BF16),
            vmem(share, BF16),
            vmem(share, BF16),
            vmem((CHIPS, ROW, E), BF16),
            vmem((CHIPS, ROW, E), BF16),
            vmem((CHIPS, ROW, E), BF16),
            vmem((CHIPS, ROW, E), BF16),
            dma((5,)),
            dma,
            dma((CHIPS,)),
            dma,
            dma,
            dma,
            dma,
            dma,
            dma,
            dma,
            dma,
            dma((6,)),
            dma((6,)),
            dma,
            dma,
            dma,
            dma,
        ],
        compiler_params=pltpu.CompilerParams(collective_id=0, has_side_effects=True),
    )(queries, ids, teacher, passages)


def shards(queries, passages, candidates, teacher):
    teacher_exp = jnp.exp(teacher)
    teacher_sum = jnp.sum(teacher_exp, -1, keepdims=True)
    entropy = jnp.sum(teacher_exp / teacher_sum * (teacher - jnp.log(teacher_sum)), -1)
    total_terms, grad_queries, grad_passages = step(
        queries.reshape(ROW, E), candidates.reshape(1, ROW), teacher.reshape(1, ROW), passages
    )
    begin = lax.axis_index("psg") * QD
    pair_loss = entropy + lax.dynamic_slice(total_terms, (0, begin), (1, QD))[0]
    return pair_loss, grad_queries.reshape(QD, QT, E), grad_passages


def solution(mesh):
    placed = (
        P(("psg", "qry"), None, None),
        P("psg", None, None),
        P(("psg", "qry"), None),
        P(("psg", "qry"), None),
    )
    return jax.shard_map(
        shards,
        mesh=mesh,
        in_specs=placed,
        out_specs=(P(("psg", "qry")), P(("psg", "qry"), None, None), P("psg", "qry", None)),
        check_vma=False,
    )
```

time: 388 us -> 75.6 us (0.19)
  waiting for transfers between devices: 140 us -> 0 us
  matrix products: 129 us -> 0 us
  Pallas kernels: 0 us -> 65.8 us
  local copies, waits for them, and re-layouts: 53 us -> 5.8 us
  starting transfers between devices: 19.1 us -> 0 us
  other arithmetic: 20.3 us -> 2.93 us
  between operations: 14 us -> 0.65 us
  loops' own time: 10.6 us -> 0 us
    dot_general x50 -> x0, matrix products: 129 us -> none  [the longest x10 66.4 us: add_rows(): jnp.einsum('sr,sx->rx', placer, flat_delta, precision=lax.Precision.HIGHEST)]
    reduce_scatter x2 -> x0, waiting for transfers between devices: 98.2 us -> none  [the longest x1 67 us: shards(): lax.psum_scatter(query_accum.astype(jnp.bfloat16), 'psg', scatter_dimensi...]
    pallas_call x0 -> x1, Pallas kernels: none -> 65.8 us  [step(): pl.pallas_call(kernel, out_shape=(jax.ShapeDtypeStruct((1, ROW), F32), ja...]
    while x62 -> x0, local copies, waits for them, and re-layouts: 40.9 us -> none
    all_gather x1 -> x0, waiting for transfers between devices: 27.6 us -> none  [shards(): query_rows = lax.all_gather(query_norm, 'psg', axis=0, tiled=True)]
    all_to_all x3 -> x0, starting transfers between devices: 19 us -> none  [the longest x1 9.59 us: shards(): lax.all_to_all(send_code, 'psg', split_axis=0, concat_axis=0, tiled=True)]
    all_to_all x3 -> x0, waiting for transfers between devices: 14.5 us -> none  [the longest x1 6.94 us: shards(): lax.all_to_all(send_grad.reshape(owner_count, capacity), 'psg', split_axi...]
    mul x5 -> x0, other arithmetic: 12.1 us -> none  [the longest x1 6.32 us: shards(): unit_slice * jnp.sum(unit_slice * unit_passage_grad, -1, keepdims=True)]
  transfers between devices with their start and end apart: 6 -> 0, of which waited for: 6 -> 0; matrix products, arithmetic and copies ran while one was open for 5% -> 0% of each run, Pallas kernels for 0% -> 0%
where the time goes in v1:
time: 75.6 us; the launch traced here: 75.2 us
  Pallas kernels  65.8 us (87%)
  local copies, waits for them, and re-layouts  5.8 us (8%)
  other arithmetic  2.93 us (4%)
    pallas_call x1, Pallas kernels, step(): pl.pallas_call(kernel, out_shape=(jax.ShapeDtypeStruct((1, ROW), F32), ja...  65.8 us
    unnamed x2, local copies, waits for them, and re-layouts  3.24 us

profile of v1, /device:TPU:1, one launch (start us, length us, event | category | flops | bytes accessed | tf_op | source)
XLA Modules:
  0.0 75.2 jit_solution(17656210546390129308)
XLA Ops:
  0.6 0.8 %exponential_reduce_fusion = f32[4]{0:T(128)S(1)} fusion(f32[4,32]{1,0:T(4,128)} %param.7), kind=kLoop, calls=%fused_computation.2 | loop fusion | flops 124 | bytes 528 | tf_op jit(solution)/shard_map/reduce_sum | solution.py:533
  1.4 0.9 %fusion = f32[4]{0:T(128)S(1)} fusion(f32[4,32]{1,0:T(4,128)} %param.7, f32[4]{0:T(128)S(1)} %log.8, f32[4]{0:T(128)S(1)} %exponential_reduce_fusion), kind=kLoop, calls=%fused_computation.1 | loop fusion | flops 508 | bytes 560 | tf_op jit(solution)/shard_map/reduce_sum | solution.py:534
  2.3 1.3 %reshape.24.ids_ref = s32[1,128]{1,0:T(1,128)} reshape(s32[4,32]{1,0:T(4,128)} %param.6) | data formatting | bytes 1024 | tf_op jit(solution)/shard_map/reshape | solution.py:536
  3.6 1.3 %reshape.25.teacher_ref = f32[1,128]{1,0:T(1,128)} reshape(f32[4,32]{1,0:T(4,128)} %param.7) | data formatting | bytes 1024 | tf_op jit(solution)/shard_map/reshape | solution.py:536
  4.9 65.8 %shard_map.67 = (f32[1,128]{1,0:T(1,128)}, bf16[128,128]{1,0:T(8,128)(2,1)}, bf16[32,64,128]{2,1,0:T(8,128)(2,1)}) custom-call(bf16[128,128]{1,0:T(8,128)(2,1)} %bitcast.4, s32[1,128]{1,0:T(1,128)} %reshape.24.ids_ref, f32[1,128]{1,0:T(1,128)} %reshape.25.teacher_ref, bf16[32,256,128]{2,1,0:T(8,128)(2,1)} %passages_hbm.1), custom_call_target="tpu_custom_call" | custom-call | tf_op jit(solution)/shard_map/pallas_call | solution.py:468
  70.7 1.3 %bitcast_add_fusion = f32[4]{0:T(128)} fusion(f32[4]{0:T(128)S(1)} %fusion, f32[1,128]{1,0:T(1,128)} %get-tuple-element.6, s32[]{:T(128)S(6)} %select_n.3), kind=kLoop, calls=%fused_computation.3 | loop fusion | flops 4 | bytes 52 | tf_op jit(solution)/shard_map/add | solution.py:539
  72.0 1.4 %copy.9 = bf16[4,32,128]{2,1,0:T(8,128)(2,1)} copy(bf16[4,32,128]{2,1,0:T(8,128)(2,1)} %bitcast.5) | data formatting | bytes 65536
  73.4 1.9 %copy.10 = bf16[32,64,128]{2,1,0:T(8,128)(2,1)} copy(bf16[32,64,128]{2,1,0:T(8,128)(2,1)} %get-tuple-element.14) | data formatting | bytes 1048576
  (1 shorter events, 0.0 us)
